TPU v7x, 128 devices: a whole 4x4x4 slice. The times are simulated.
128 devices in a mesh: row: 16 (over y, z), col: 8 (over x, core).
Axes of the slice: x: 4, y: 4, z: 4, core: 2. Of those that a mesh axis runs over, the one named last changes fastest.
Arguments:
- block_cols: int32 [64, 16], replicated, may hold values from -1 to 63, as said below
- step_dir: bfloat16 [64, 16, 128, 128], P('row', 'col')
- intersection: bfloat16 [64, 16, 128, 128], P('row', 'col')
- density: bfloat16 [64, 16, 128, 128], P('row', 'col')
- kohn_sham: bfloat16 [64, 16, 128, 128], P('row', 'col')
Outputs:
- commutator: bfloat16 [64, 16, 128, 128], P('row', 'col')
- trace_value: float32 [], replicated
Inputs may be any that keep to these rules, and one draw needn't show every extreme that they name: block_cols[i, s] is -1 or a block column of group s // 2, that is from (s // 2) * 8 to (s // 2 + 1) * 8 - 1; the live entries of one block row within one group are distinct; the pattern is symmetric (j is live in row i exactly when i is live in row j) and holds every diagonal block.
All inputs are finite; a program needn't handle non-finite values.
Results may differ from a plain program's by a relative error of at most 0.0057.
Values may be sent and summed in bfloat16 or wider, within the bound.
A program may use at most 64 MiB of HBM per device.

v0:
```python
import jax
import jax.numpy as jnp
from jax import lax
from jax.sharding import PartitionSpec as P


def per_device(block_cols, step_dir, intersection, density, kohn_sham):
    row_total = step_dir.shape[0]
    slot_total = step_dir.shape[1]
    block_size = step_dir.shape[2]
    col_groups = lax.axis_size("col")
    blocks_total = block_cols.shape[0]
    row_index = lax.axis_index("row")
    col_index = lax.axis_index("col")
    own_rows = lax.dynamic_slice_in_dim(block_cols, row_index * row_total, row_total, 0)
    own_cols = lax.dynamic_slice_in_dim(own_rows, col_index * slot_total, slot_total, 1)
    group_cols = lax.dynamic_slice_in_dim(block_cols, col_index * slot_total, slot_total, 1)
    left_live = own_cols >= 0
    targets = own_rows.reshape(row_total, col_groups, slot_total).transpose(1, 0, 2)

    def partial_blocks(left_blocks, gathered, wanted):
        safe_rows = jnp.clip(wanted, 0, blocks_total - 1)
        right_rows = gathered[safe_rows]
        right_cols = group_cols[safe_rows]
        matched = (
            (right_cols[:, :, :, None, :] == own_cols[None, :, None, :, None])
            & left_live[None, :, None, :, None]
            & (wanted >= 0)[:, :, :, None, None]
        )
        picked = jnp.where(
            matched[..., None, None],
            right_rows[:, :, :, None, :, :, :],
            jnp.zeros((), jnp.bfloat16),
        ).sum(axis=4)
        terms = jnp.einsum(
            "iapr,gisaqr->gispq", left_blocks, picked, preferred_element_type=jnp.float32
        )
        group_count = wanted.shape[0]
        return terms.reshape(group_count * row_total, slot_total, block_size, block_size)

    def product(left_blocks, right_blocks):
        gathered = lax.all_gather(right_blocks, "row", axis=0, tiled=True)
        return lax.psum_scatter(
            partial_blocks(left_blocks, gathered, targets), "col", scatter_dimension=0, tiled=True
        )

    scaled_step = product(step_dir, intersection).astype(jnp.bfloat16)
    change = (-(product(scaled_step, density) + product(density, scaled_step))).astype(jnp.bfloat16)
    commutator = (product(kohn_sham, change) - product(change, kohn_sham)).astype(jnp.bfloat16)
    local_trace = jnp.sum(change.astype(jnp.float32) * kohn_sham.astype(jnp.float32))
    trace_value = lax.psum(local_trace, ("row", "col")) / (blocks_total * block_size * block_size)
    return (commutator, trace_value)


def solution(mesh):
    in_specs = (
        P(),
        P("row", "col", None, None),
        P("row", "col", None, None),
        P("row", "col", None, None),
        P("row", "col", None, None),
    )
    out_specs = (P("row", "col", None, None), P())
    return jax.shard_map(
        per_device, mesh=mesh, in_specs=in_specs, out_specs=out_specs, check_vma=False
    )
```

profile of v0, /device:TPU:1, one launch (start us, length us, event | category | flops | bytes accessed | tf_op | source)
XLA Modules:
  0.0 501.8 jit_solution(6847474959793263105)
XLA Ops:
  9.5 0.8 broadcast_compare_fusion
  10.4 0.8 dynamic-slice_compare_fusion
  11.4 0.8 dynamic-slice_clamp_fusion
  14.0 50.7 %all-gather.14.cloned.1.call-done = bf16[64,2,128,128]{3,2,1,0:T(8,128)(2,1)} async-done(((bf16[4,2,128,128]{3,2,1,0:T(8,128)(2,1)}), bf16[64,2,128,128]{3,2,1,0:T(8,128)(2,1)}) %all-gather.14.cloned.1.call-update) | async-done | bytes 4194320 | tf_op jit(solution)/shard_map/all_gather | solution.py:42
  64.7 5.2 %gather_fusion.5 = bf16[64,2,128,128]{3,2,1,0:T(8,128)(2,1)} fusion(bf16[64,2,128,128]{3,2,1,0:T(8,128)(2,1)} %all-gather.14.cloned.1.call-done, s32[1024]{0:T(1024)S(1)} %pad_clamp_fusion), kind=kCustom, calls=%fused_computation.5 | custom fusion | bytes 8388864 | tf_op jit(solution)/shard_map/gather | solution.py:23
  69.9 48.0 %all-gather.8.cloned.1.call-done = bf16[64,2,128,128]{3,2,1,0:T(8,128)(2,1)} async-done(((bf16[4,2,128,128]{3,2,1,0:T(8,128)(2,1)}), bf16[64,2,128,128]{3,2,1,0:T(8,128)(2,1)}) %all-gather.8.cloned.1.call-update) | async-done | bytes 4194320 | tf_op jit(solution)/shard_map/all_gather | solution.py:42
  118.0 5.2 %gather_fusion.2 = bf16[64,2,128,128]{3,2,1,0:T(8,128)(2,1)} fusion(bf16[64,2,128,128]{3,2,1,0:T(8,128)(2,1)} %all-gather.8.cloned.1.call-done, s32[1024]{0:T(1024)S(1)} %pad_clamp_fusion), kind=kCustom, calls=%fused_computation.2 | custom fusion | bytes 8388864 | tf_op jit(solution)/shard_map/gather | solution.py:23
  123.2 48.1 %all-gather.6.cloned.1.call-done = bf16[64,2,128,128]{3,2,1,0:T(8,128)(2,1)} async-done(((bf16[4,2,128,128]{3,2,1,0:T(8,128)(2,1)}), bf16[64,2,128,128]{3,2,1,0:T(8,128)(2,1)}) %all-gather.6.cloned.1.call-update) | async-done | bytes 4194320 | tf_op jit(solution)/shard_map/all_gather | solution.py:42
  171.2 5.2 %gather_fusion.1 = bf16[64,2,128,128]{3,2,1,0:T(8,128)(2,1)} fusion(bf16[64,2,128,128]{3,2,1,0:T(8,128)(2,1)} %all-gather.6.cloned.1.call-done, s32[1024]{0:T(1024)S(1)} %pad_clamp_fusion), kind=kCustom, calls=%fused_computation.1 | custom fusion | bytes 8388864 | tf_op jit(solution)/shard_map/gather | solution.py:23
  176.5 17.5 %select_reduce_fusion = (bf16[8,4,2,2,128,128]{5,4,3,2,1,0:T(8,128)(2,1)}, bf16[8,4,2,2,128,128]{5,4,3,2,1,0:T(8,128)(2,1)S(1)}, bf16[8,4,2,2,128,128]{5,4,3,2,1,0:T(8,128)(2,1)}) fusion(pred[8,4,2,2,2]{4,3,2,1,0:T(4,128)(4,1)S(1)} %and_and_fusion, bf16[8,4,2,2,128,128]{5,4,3,2,1,0:T(8,128)(2,1)} %bitcast.70, bf16[8,4,2,2,128,128]{5,4,3,2,1,0:T(8,128)(2,1)} %bitcast.71, ...), kind=kLoop, calls=%fused_computation.6 | loop fusion | flops 18874368 | bytes 25166080 | tf_op jit(solution)/shard_map/reduce_sum | solution.py:34
  193.9 3.2 fusion.11
  197.1 5.4 %copy.48 = f32[8,4,2,128,128]{4,3,2,1,0:T(8,128)} copy(f32[8,4,2,128,128]{3,4,2,0,1:T(8,128)} %fusion.11) | data formatting | bytes 8388608 | tf_op jit(solution)/shard_map/iapr,gisaqr->gispq/transpose | solution.py:35
  202.6 34.9 %reduce-scatter.5.cloned.1.call-done = f32[4,2,128,128]{3,2,1,0:T(8,128)} async-done(((f32[32,2,128,128]{3,2,1,0:T(8,128)}), f32[4,2,128,128]{3,2,1,0:T(8,128)}) %reduce-scatter.5.cloned.1.call-update) | async-done | bytes 524304 | tf_op jit(solution)/shard_map/reduce_scatter | solution.py:43
  237.4 1.8 convert_element_type.10
  239.5 53.7 %all-gather.10.cloned.1.call-done = bf16[64,2,128,128]{3,2,1,0:T(8,128)(2,1)} async-done(((bf16[4,2,128,128]{3,2,1,0:T(8,128)(2,1)}), bf16[64,2,128,128]{3,2,1,0:T(8,128)(2,1)}) %all-gather.10.cloned.1.call-update) | async-done | bytes 4194320 | tf_op jit(solution)/shard_map/all_gather | solution.py:42
  293.2 5.2 %gather_fusion.3 = bf16[64,2,128,128]{3,2,1,0:T(8,128)(2,1)} fusion(bf16[64,2,128,128]{3,2,1,0:T(8,128)(2,1)} %all-gather.10.cloned.1.call-done, s32[1024]{0:T(1024)S(1)} %pad_clamp_fusion), kind=kCustom, calls=%fused_computation.3 | custom fusion | bytes 8388864 | tf_op jit(solution)/shard_map/gather | solution.py:23
  298.4 6.2 %select_reduce_fusion.2 = bf16[8,4,2,2,128,128]{5,4,3,2,1,0:T(8,128)(2,1)S(1)} fusion(pred[8,4,2,2,2]{4,3,2,1,0:T(4,128)(4,1)S(1)} %and_and_fusion, bf16[8,4,2,2,128,128]{5,4,3,2,1,0:T(8,128)(2,1)} %bitcast.69), kind=kLoop, calls=%fused_computation.8 | loop fusion | flops 6291456 | bytes 8388864 | tf_op jit(solution)/shard_map/reduce_sum | solution.py:34
  304.6 1.3 fusion.5
  305.9 0.9 copy-done.2
  306.8 3.2 fusion
  310.0 5.4 %copy.51 = f32[8,4,2,128,128]{4,3,2,1,0:T(8,128)} copy(f32[8,4,2,128,128]{3,4,2,0,1:T(8,128)} %fusion) | data formatting | bytes 8388608 | tf_op jit(solution)/shard_map/add | solution.py:48
  315.5 34.8 %reduce-scatter.11.cloned.1.call-done = f32[4,2,128,128]{3,2,1,0:T(8,128)} async-done(((f32[32,2,128,128]{3,2,1,0:T(8,128)}), f32[4,2,128,128]{3,2,1,0:T(8,128)}) %reduce-scatter.11.cloned.1.call-update) | async-done | bytes 524304 | tf_op jit(solution)/shard_map/reduce_scatter | solution.py:43
  350.3 2.4 multiply_reduce_fusion
  352.8 5.4 %fusion.17 = f32[8,4,2,128,128]{3,4,2,0,1:T(8,128)} fusion(bf16[8,4,2,2,128,128]{5,4,3,2,1,0:T(8,128)(2,1)} %get-tuple-element.2, bf16[4,2,128,128]{3,2,1,0:T(8,128)(2,1)} %get-tuple-element.6), kind=kOutput, calls=%fused_computation.25 | convolution fusion | flops 536870912 | bytes 8650752 | tf_op jit(solution)/shard_map/iapr,gisaqr->gispq/dot_general | solution.py:35
  358.2 5.4 %copy.55 = f32[8,4,2,128,128]{4,3,2,1,0:T(8,128)} copy(f32[8,4,2,128,128]{3,4,2,0,1:T(8,128)} %fusion.17) | data formatting | bytes 8388608 | tf_op jit(solution)/shard_map/iapr,gisaqr->gispq/transpose | solution.py:35
  363.6 42.6 %all-gather.12.cloned.1.call-done = bf16[64,2,128,128]{3,2,1,0:T(8,128)(2,1)} async-done(((bf16[4,2,128,128]{3,2,1,0:T(8,128)(2,1)}), bf16[64,2,128,128]{3,2,1,0:T(8,128)(2,1)}) %all-gather.12.cloned.1.call-update) | async-done | bytes 4194320 | tf_op jit(solution)/shard_map/all_gather | solution.py:42
  406.2 5.2 %gather_fusion.4 = bf16[64,2,128,128]{3,2,1,0:T(8,128)(2,1)} fusion(bf16[64,2,128,128]{3,2,1,0:T(8,128)(2,1)} %all-gather.12.cloned.1.call-done, s32[1024]{0:T(1024)S(1)} %pad_clamp_fusion), kind=kCustom, calls=%fused_computation.4 | custom fusion | bytes 8388864 | tf_op jit(solution)/shard_map/gather | solution.py:23
  411.5 6.2 %select_reduce_fusion.1 = bf16[8,4,2,2,128,128]{5,4,3,2,1,0:T(8,128)(2,1)S(1)} fusion(pred[8,4,2,2,2]{4,3,2,1,0:T(4,128)(4,1)S(1)} %and_and_fusion, bf16[8,4,2,2,128,128]{5,4,3,2,1,0:T(8,128)(2,1)} %bitcast.68), kind=kLoop, calls=%fused_computation.7 | loop fusion | flops 6291456 | bytes 8388864 | tf_op jit(solution)/shard_map/reduce_sum | solution.py:34
  417.6 3.2 fusion.14
  420.8 5.5 %copy.53 = f32[8,4,2,128,128]{4,3,2,1,0:T(8,128)} copy(f32[8,4,2,128,128]{3,4,2,0,1:T(8,128)} %fusion.14) | data formatting | bytes 8388608 | tf_op jit(solution)/shard_map/iapr,gisaqr->gispq/transpose | solution.py:35
  426.4 65.1 %psum.7 = f32[]{:T(128)} all-reduce(f32[]{:T(128)} %get-tuple-element.5), channel_id=1, replica_groups=mesh['row'=16,'col'=8] {'row','col'}, use_global_device_ids=true, to_apply=%region_11.12 | all-reduce | flops 1 | bytes 8 | tf_op jit(solution)/shard_map/psum | solution.py:51
  492.2 2.0 subtract_convert_fusion
  (44 shorter events, 5.0 us)
Async XLA Ops:
  7.2 186.8 %copy-start = (bf16[4,2,128,128]{3,2,1,0:T(8,128)(2,1)S(1)}, bf16[4,2,128,128]{3,2,1,0:T(8,128)(2,1)}, u32[]{:S(2)}) copy-start(bf16[4,2,128,128]{3,2,1,0:T(8,128)(2,1)} %param.6) | copy-start | bytes 786436
  7.2 57.5 %all-gather.14.cloned.1.call-start = ((), (), s32[]{:S(2)}) async-start(), calls=%async_computation.10 | async-start | bytes 4456448 | tf_op jit(solution)/shard_map/all_gather | solution.py:42
  7.9 110.1 %all-gather.8.cloned.1.call-start = ((), (), s32[]{:S(2)}) async-start(), calls=%async_computation.5 | async-start | bytes 4456448 | tf_op jit(solution)/shard_map/all_gather | solution.py:42
  8.7 162.6 %all-gather.6.cloned.1.call-start = ((), (), s32[]{:S(2)}) async-start(), calls=%async_computation.4 | async-start | bytes 4456448 | tf_op jit(solution)/shard_map/all_gather | solution.py:42
  9.4 228.0 %reduce-scatter.5.cloned.1.call-start = ((), (), s32[]{:S(2)}) async-start(), calls=%async_computation.6 | async-start | bytes 4718592 | tf_op jit(solution)/shard_map/reduce_scatter | solution.py:43
  202.5 90.7 %all-gather.10.cloned.1.call-start = ((), (), s32[]{:S(2)}) async-start(), calls=%async_computation.7 | async-start | bytes 4456448 | tf_op jit(solution)/shard_map/all_gather | solution.py:42
  239.2 111.0 %reduce-scatter.11.cloned.1.call-start = ((), (), s32[]{:S(2)}) async-start(), calls=%async_computation.12 | async-start | bytes 4718592 | tf_op jit(solution)/shard_map/reduce_scatter | solution.py:43
  298.4 6.2 %copy-start.4 = (bf16[4,2,128,128]{3,2,1,0:T(8,128)(2,1)S(1)}, bf16[4,2,128,128]{3,2,1,0:T(8,128)(2,1)}, u32[]{:S(2)}) copy-start(bf16[4,2,128,128]{3,2,1,0:T(8,128)(2,1)} %param.8) | copy-start | bytes 786436
  304.6 2.2 copy-start.2
  304.6 2.2 copy-start.3
  315.4 34.9 %copy-start.5 = (bf16[4,2,128,128]{3,2,1,0:T(8,128)(2,1)S(1)}, bf16[4,2,128,128]{3,2,1,0:T(8,128)(2,1)}, u32[]{:S(2)}) copy-start(bf16[4,2,128,128]{3,2,1,0:T(8,128)(2,1)} %param.9) | copy-start | bytes 786436
  315.4 90.8 %all-gather.12.cloned.1.call-start = ((), (), s32[]{:S(2)}) async-start(), calls=%async_computation.8 | async-start | bytes 4456448 | tf_op jit(solution)/shard_map/all_gather | solution.py:42
  352.7 139.4 %reduce-scatter.9.cloned.1.call-start = ((), (), s32[]{:S(2)}) async-start(), calls=%async_computation.11 | async-start | bytes 4718592 | tf_op jit(solution)/shard_map/reduce_scatter | solution.py:43
  363.6 128.6 %reduce-scatter.7.cloned.1.call-start = ((), (), s32[]{:S(2)}) async-start(), calls=%async_computation.9 | async-start | bytes 4718592 | tf_op jit(solution)/shard_map/reduce_scatter | solution.py:43
  420.8 73.3 %copy-start.1 = (bf16[4,2,128,128]{3,2,1,0:T(8,128)(2,1)S(1)}, bf16[4,2,128,128]{3,2,1,0:T(8,128)(2,1)}, u32[]{:S(2)}) copy-start(bf16[4,2,128,128]{3,2,1,0:T(8,128)(2,1)} %param.6) | copy-start | bytes 786436
Sparse Core Ops, SparseCore 0:
  10.1 54.5 all-gather.13
  66.8 51.0 all-gather.7
  120.1 51.0 all-gather.5
  202.6 34.7 reduce-scatter.4
  240.0 53.1 all-gather.9
  315.5 34.6 reduce-scatter.10
  353.0 53.2 all-gather.11
  408.6 35.0 reduce-scatter.8
  446.1 37.3 reduce-scatter.6
where the time goes:
time: 503 us; the launch traced here: 502 us
  waiting for transfers between devices  315 us (63%)
  blocking collectives  65.1 us (13%)
  local copies, waits for them, and re-layouts  50.7 us (10%)
  other arithmetic  38.5 us (8%)
  matrix products  16.3 us (3%)
  between operations  15.7 us (3%)
    all_gather x5, waiting for transfers between devices, product(): gathered = lax.all_gather(right_blocks, 'row', axis=0, tiled=True)  243 us
    reduce_scatter x4, waiting for transfers between devices, product(): lax.psum_scatter(partial_blocks(left_blocks, gathered, targets), 'col', s...  69.7 us
    psum x1, blocking collectives, per_device(): lax.psum(local_trace, ('row', 'col'))  65.1 us
    reduce_sum x3, other arithmetic, partial_blocks(): picked = jnp.where(matched[..., None, None], right_rows[:, :, :, None, :,...  29.8 us
    gather x5, local copies, waits for them, and re-layouts, partial_blocks(): right_rows = gathered[safe_rows]  26.1 us
    dot_general x5, matrix products, partial_blocks(): jnp.einsum('iapr,gisaqr->gispq', left_blocks, picked, preferred_element_t...  16.3 us
    transpose x3, local copies, waits for them, and re-layouts, partial_blocks(): jnp.einsum('iapr,gisaqr->gispq', left_blocks, picked, preferred_element_t...  16.2 us
  transfers between devices with their start and end apart: 9, of which 7 were waited for; matrix products, arithmetic and copies ran while one was open for 9% of the time, Pallas kernels for 0%

commit v1 on v0

--- a/solution.py
+++ b/solution.py
@@ -39,7 +39,14 @@
         return terms.reshape(group_count * row_total, slot_total, block_size, block_size)
 
     def product(left_blocks, right_blocks):
-        gathered = lax.all_gather(right_blocks, "row", axis=0, tiled=True)
+        inbox = [right_blocks]
+        num = jax.lax.axis_size("row")
+        for m in range(num - 1):
+            known = jax.lax.ppermute(inbox[-1], "row", [(j0, (j0 + 1) % num) for j0 in range(num)])
+            inbox.append(known)
+        y_new = jnp.concatenate(inbox[::-1], axis=0)
+        current_value = jax.lax.axis_index("row")
+        gathered = jnp.roll(y_new, (current_value + 1) * right_blocks.shape[0], axis=0)
         return lax.psum_scatter(
             partial_blocks(left_blocks, gathered, targets), "col", scatter_dimension=0, tiled=True
         )

time: 503 us -> 873 us (1.74); the launches traced: 502 us -> 863 us
  waiting for transfers between devices: 315 us -> 600 us
  local copies, waits for them, and re-layouts: 50.7 us -> 85.2 us
  blocking collectives: 65.1 us -> 81.6 us
  other arithmetic: 38.5 us -> 53.3 us
  starting transfers between devices: 0.54 us -> 9.32 us
    ppermute x0 -> x75, waiting for transfers between devices: none -> 516 us  [product(): jax.lax.ppermute(inbox[-1], 'row', [(j0, (j0 + 1) % num) for j0 in range(...]
    all_gather x5 -> x0, waiting for transfers between devices: 243 us -> none  [product(): gathered = lax.all_gather(right_blocks, 'row', axis=0, tiled=True)]
    unnamed x13 -> x154, local copies, waits for them, and re-layouts: 1.06 us -> 34.3 us
    psum x1, blocking collectives: 65.1 us -> 81.6 us  [per_device(): lax.psum(local_trace, ('row', 'col'))]
    concatenate x0 -> x5, other arithmetic: none -> 15.8 us  [the longest x4 15.7 us: product(): jnp.roll(y_new, (current_value + 1) * right_blocks.shape[0], axis=0)]
    reduce_scatter x4, waiting for transfers between devices: 69.7 us -> 84.2 us  [product(): lax.psum_scatter(partial_blocks(left_blocks, gathered, targets), 'col', s...]
    ppermute x0 -> x75, starting transfers between devices: none -> 9.16 us  [product(): jax.lax.ppermute(inbox[-1], 'row', [(j0, (j0 + 1) % num) for j0 in range(...]
  transfers between devices with their start and end apart: 9 -> 79, of which waited for: 7 -> 75; matrix products, arithmetic and copies ran while one was open for 9% -> 7% of each run, Pallas kernels for 0% -> 0%
where the time goes in v1:
time: 873 us; the launch traced here: 863 us
  waiting for transfers between devices  600 us (69%)
  local copies, waits for them, and re-layouts  85.2 us (10%)
  blocking collectives  81.6 us (9%)
  other arithmetic  53.3 us (6%)
  between operations  16.8 us (2%)
  matrix products  16.6 us (2%)
  starting transfers between devices  9.32 us (1%)
    ppermute x75, waiting for transfers between devices, product(): jax.lax.ppermute(inbox[-1], 'row', [(j0, (j0 + 1) % num) for j0 in range(...  516 us
    reduce_scatter x4, waiting for transfers between devices, product(): lax.psum_scatter(partial_blocks(left_blocks, gathered, targets), 'col', s...  84.2 us
    psum x1, blocking collectives, per_device(): lax.psum(local_trace, ('row', 'col'))  81.6 us
    unnamed x154, local copies, waits for them, and re-layouts  34.3 us
    reduce_sum x3, other arithmetic, partial_blocks(): picked = jnp.where(matched[..., None, None], right_rows[:, :, :, None, :,...  30.1 us
    gather x5, local copies, waits for them, and re-layouts, partial_blocks(): right_rows = gathered[safe_rows]  26.4 us
  transfers between devices with their start and end apart: 79, of which 75 were waited for; matrix products, arithmetic and copies ran while one was open for 7% of the time, Pallas kernels for 0%

profile of v1, /device:TPU:1, one launch (start us, length us, event | category | flops | bytes accessed | tf_op | source)
XLA Modules:
  0.0 862.9 jit_solution(6821174722717358307)
XLA Ops:
  313.2 17.8 %select_reduce_fusion = (bf16[8,4,2,2,128,128]{5,4,3,2,1,0:T(8,128)(2,1)}, bf16[8,4,2,2,128,128]{5,4,3,2,1,0:T(8,128)(2,1)S(1)}, bf16[8,4,2,2,128,128]{5,4,3,2,1,0:T(8,128)(2,1)}) fusion(pred[8,4,2,2,2]{4,3,2,1,0:T(4,128)(4,1)S(1)} %and_and_fusion, bf16[8,4,2,2,128,128]{5,4,3,2,1,0:T(8,128)(2,1)} %bitcast.71, bf16[8,4,2,2,128,128]{5,4,3,2,1,0:T(8,128)(2,1)} %bitcast.72, ...), kind=kLoop, calls=%fused_computation.16 | loop fusion | flops 18874368 | bytes 25166080 | tf_op jit(solution)/shard_map/reduce_sum | solution.py:34
  339.6 34.5 %reduce-scatter.5.cloned.1.call-done = f32[4,2,128,128]{3,2,1,0:T(8,128)} async-done(((f32[32,2,128,128]{3,2,1,0:T(8,128)}), f32[4,2,128,128]{3,2,1,0:T(8,128)}) %reduce-scatter.5.cloned.1.call-update) | async-done | bytes 524304 | tf_op jit(solution)/shard_map/reduce_scatter | solution.py:50
  383.9 8.5 collective-permute-done.31
  392.4 8.5 collective-permute-done.32
  401.0 9.1 %collective-permute-done.33 = bf16[4,2,128,128]{3,2,1,0:T(8,128)(2,1)S(1)} collective-permute-done((bf16[4,2,128,128]{3,2,1,0:T(8,128)(2,1)S(1)}, bf16[4,2,128,128]{3,2,1,0:T(8,128)(2,1)S(1)}, u32[]{:S(2)}, u32[]{:S(2)}) %collective-permute-start.33) | collective-permute-done | bytes 262176 | tf_op jit(solution)/shard_map/ppermute | solution.py:45
  410.1 10.3 %collective-permute-done.34 = bf16[4,2,128,128]{3,2,1,0:T(8,128)(2,1)S(1)} collective-permute-done((bf16[4,2,128,128]{3,2,1,0:T(8,128)(2,1)S(1)}, bf16[4,2,128,128]{3,2,1,0:T(8,128)(2,1)S(1)}, u32[]{:S(2)}, u32[]{:S(2)}) %collective-permute-start.34) | collective-permute-done | bytes 262176 | tf_op jit(solution)/shard_map/ppermute | solution.py:45
  420.4 11.6 %collective-permute-done.35 = bf16[4,2,128,128]{3,2,1,0:T(8,128)(2,1)S(1)} collective-permute-done((bf16[4,2,128,128]{3,2,1,0:T(8,128)(2,1)S(1)}, bf16[4,2,128,128]{3,2,1,0:T(8,128)(2,1)S(1)}, u32[]{:S(2)}, u32[]{:S(2)}) %collective-permute-start.35) | collective-permute-done | bytes 262176 | tf_op jit(solution)/shard_map/ppermute | solution.py:45
  432.0 10.7 %collective-permute-done.36 = bf16[4,2,128,128]{3,2,1,0:T(8,128)(2,1)S(1)} collective-permute-done((bf16[4,2,128,128]{3,2,1,0:T(8,128)(2,1)S(1)}, bf16[4,2,128,128]{3,2,1,0:T(8,128)(2,1)S(1)}, u32[]{:S(2)}, u32[]{:S(2)}) %collective-permute-start.36) | collective-permute-done | bytes 262176 | tf_op jit(solution)/shard_map/ppermute | solution.py:45
  442.7 9.8 %collective-permute-done.37 = bf16[4,2,128,128]{3,2,1,0:T(8,128)(2,1)S(1)} collective-permute-done((bf16[4,2,128,128]{3,2,1,0:T(8,128)(2,1)S(1)}, bf16[4,2,128,128]{3,2,1,0:T(8,128)(2,1)S(1)}, u32[]{:S(2)}, u32[]{:S(2)}) %collective-permute-start.37) | collective-permute-done | bytes 262176 | tf_op jit(solution)/shard_map/ppermute | solution.py:45
  452.5 9.0 %collective-permute-done.38 = bf16[4,2,128,128]{3,2,1,0:T(8,128)(2,1)S(1)} collective-permute-done((bf16[4,2,128,128]{3,2,1,0:T(8,128)(2,1)S(1)}, bf16[4,2,128,128]{3,2,1,0:T(8,128)(2,1)S(1)}, u32[]{:S(2)}, u32[]{:S(2)}) %collective-permute-start.38) | collective-permute-done | bytes 262176 | tf_op jit(solution)/shard_map/ppermute | solution.py:45
  461.5 8.5 collective-permute-done.39
  470.0 8.5 collective-permute-done.40
  478.6 8.5 collective-permute-done.41
  487.1 8.6 collective-permute-done.42
  495.7 9.8 %collective-permute-done.43 = bf16[4,2,128,128]{3,2,1,0:T(8,128)(2,1)S(1)} collective-permute-done((bf16[4,2,128,128]{3,2,1,0:T(8,128)(2,1)S(1)}, bf16[4,2,128,128]{3,2,1,0:T(8,128)(2,1)S(1)}, u32[]{:S(2)}, u32[]{:S(2)}) %collective-permute-start.43) | collective-permute-done | bytes 262176 | tf_op jit(solution)/shard_map/ppermute | solution.py:45
  505.5 10.9 %collective-permute-done.44 = bf16[4,2,128,128]{3,2,1,0:T(8,128)(2,1)S(1)} collective-permute-done((bf16[4,2,128,128]{3,2,1,0:T(8,128)(2,1)S(1)}, bf16[4,2,128,128]{3,2,1,0:T(8,128)(2,1)S(1)}, u32[]{:S(2)}, u32[]{:S(2)}) %collective-permute-start.44) | collective-permute-done | bytes 262176 | tf_op jit(solution)/shard_map/ppermute | solution.py:45
  542.7 49.7 %reduce-scatter.11.cloned.1.call-done = f32[4,2,128,128]{3,2,1,0:T(8,128)} async-done(((f32[32,2,128,128]{3,2,1,0:T(8,128)}), f32[4,2,128,128]{3,2,1,0:T(8,128)}) %reduce-scatter.11.cloned.1.call-update) | async-done | bytes 524304 | tf_op jit(solution)/shard_map/reduce_scatter | solution.py:50
  613.9 8.5 collective-permute-done.46
  622.4 8.5 collective-permute-done.47
  631.0 9.1 %collective-permute-done.48 = bf16[4,2,128,128]{3,2,1,0:T(8,128)(2,1)S(1)} collective-permute-done((bf16[4,2,128,128]{3,2,1,0:T(8,128)(2,1)S(1)}, bf16[4,2,128,128]{3,2,1,0:T(8,128)(2,1)S(1)}, u32[]{:S(2)}, u32[]{:S(2)}) %collective-permute-start.48) | collective-permute-done | bytes 262176 | tf_op jit(solution)/shard_map/ppermute | solution.py:45
  640.0 10.2 %collective-permute-done.49 = bf16[4,2,128,128]{3,2,1,0:T(8,128)(2,1)S(1)} collective-permute-done((bf16[4,2,128,128]{3,2,1,0:T(8,128)(2,1)S(1)}, bf16[4,2,128,128]{3,2,1,0:T(8,128)(2,1)S(1)}, u32[]{:S(2)}, u32[]{:S(2)}) %collective-permute-start.49) | collective-permute-done | bytes 262176 | tf_op jit(solution)/shard_map/ppermute | solution.py:45
  650.2 11.6 %collective-permute-done.50 = bf16[4,2,128,128]{3,2,1,0:T(8,128)(2,1)S(1)} collective-permute-done((bf16[4,2,128,128]{3,2,1,0:T(8,128)(2,1)S(1)}, bf16[4,2,128,128]{3,2,1,0:T(8,128)(2,1)S(1)}, u32[]{:S(2)}, u32[]{:S(2)}) %collective-permute-start.50) | collective-permute-done | bytes 262176 | tf_op jit(solution)/shard_map/ppermute | solution.py:45
  661.9 10.8 %collective-permute-done.51 = bf16[4,2,128,128]{3,2,1,0:T(8,128)(2,1)S(1)} collective-permute-done((bf16[4,2,128,128]{3,2,1,0:T(8,128)(2,1)S(1)}, bf16[4,2,128,128]{3,2,1,0:T(8,128)(2,1)S(1)}, u32[]{:S(2)}, u32[]{:S(2)}) %collective-permute-start.51) | collective-permute-done | bytes 262176 | tf_op jit(solution)/shard_map/ppermute | solution.py:45
  672.7 9.9 %collective-permute-done.52 = bf16[4,2,128,128]{3,2,1,0:T(8,128)(2,1)S(1)} collective-permute-done((bf16[4,2,128,128]{3,2,1,0:T(8,128)(2,1)S(1)}, bf16[4,2,128,128]{3,2,1,0:T(8,128)(2,1)S(1)}, u32[]{:S(2)}, u32[]{:S(2)}) %collective-permute-start.52) | collective-permute-done | bytes 262176 | tf_op jit(solution)/shard_map/ppermute | solution.py:45
  682.6 9.1 %collective-permute-done.53 = bf16[4,2,128,128]{3,2,1,0:T(8,128)(2,1)S(1)} collective-permute-done((bf16[4,2,128,128]{3,2,1,0:T(8,128)(2,1)S(1)}, bf16[4,2,128,128]{3,2,1,0:T(8,128)(2,1)S(1)}, u32[]{:S(2)}, u32[]{:S(2)}) %collective-permute-start.53) | collective-permute-done | bytes 262176 | tf_op jit(solution)/shard_map/ppermute | solution.py:45
  691.7 8.5 collective-permute-done.54
  700.2 8.5 collective-permute-done.55
  709.0 8.5 collective-permute-done.56
  717.5 8.5 collective-permute-done.57
  726.1 9.7 %collective-permute-done.58 = bf16[4,2,128,128]{3,2,1,0:T(8,128)(2,1)S(1)} collective-permute-done((bf16[4,2,128,128]{3,2,1,0:T(8,128)(2,1)S(1)}, bf16[4,2,128,128]{3,2,1,0:T(8,128)(2,1)S(1)}, u32[]{:S(2)}, u32[]{:S(2)}) %collective-permute-start.58) | collective-permute-done | bytes 262176 | tf_op jit(solution)/shard_map/ppermute | solution.py:45
  735.8 10.8 %collective-permute-done.59 = bf16[4,2,128,128]{3,2,1,0:T(8,128)(2,1)S(1)} collective-permute-done((bf16[4,2,128,128]{3,2,1,0:T(8,128)(2,1)S(1)}, bf16[4,2,128,128]{3,2,1,0:T(8,128)(2,1)S(1)}, u32[]{:S(2)}, u32[]{:S(2)}) %collective-permute-start.59) | collective-permute-done | bytes 262176 | tf_op jit(solution)/shard_map/ppermute | solution.py:45
  770.6 81.6 %psum.7 = f32[]{:T(128)} all-reduce(f32[]{:T(128)} %get-tuple-element.6), channel_id=1, replica_groups=mesh['row'=16,'col'=8] {'row','col'}, use_global_device_ids=true, to_apply=%region_11.13 | all-reduce | flops 1 | bytes 8 | tf_op jit(solution)/shard_map/psum | solution.py:58
  (329 shorter events, 397.7 us)
Async XLA Ops:
  7.2 366.9 %reduce-scatter.5.cloned.1.call-start = ((), (), s32[]{:S(2)}) async-start(), calls=%async_computation.4 | async-start | bytes 4718592 | tf_op jit(solution)/shard_map/reduce_scatter | solution.py:50
  11.4 20.4 %collective-permute-start.60 = (bf16[4,2,128,128]{3,2,1,0:T(8,128)(2,1)}, bf16[4,2,128,128]{3,2,1,0:T(8,128)(2,1)S(1)}, u32[]{:S(2)}, u32[]{:S(2)}) collective-permute-start(bf16[4,2,128,128]{3,2,1,0:T(8,128)(2,1)} %param.11), channel_id=1, source_target_pairs={{0,8},{8,16},{16,24},{24,32},{32,40},{40,48},{48,56},{56,64},{64,7... | collective-permute-start | bytes 786440 | tf_op jit(solution)/shard_map/ppermute | solution.py:45
  20.5 16.9 %collective-permute-start.1 = (bf16[4,2,128,128]{3,2,1,0:T(8,128)(2,1)S(1)}, bf16[4,2,128,128]{3,2,1,0:T(8,128)(2,1)S(1)}, u32[]{:S(2)}, u32[]{:S(2)}) collective-permute-start(bf16[4,2,128,128]{3,2,1,0:T(8,128)(2,1)S(1)} %collective-permute-done), channel_id=1, source_target_pairs={{0,8},{8,16},{16,24},{24,32},{32,40},{40,48},{48,56},{56,64},{64,7... | collective-permute-start | bytes 786440 | tf_op jit(solution)/shard_map/ppermute | solution.py:45
  26.2 16.9 %collective-permute-start.16 = (bf16[4,2,128,128]{3,2,1,0:T(8,128)(2,1)S(1)}, bf16[4,2,128,128]{3,2,1,0:T(8,128)(2,1)S(1)}, u32[]{:S(2)}, u32[]{:S(2)}) collective-permute-start(bf16[4,2,128,128]{3,2,1,0:T(8,128)(2,1)S(1)} %collective-permute-done.15), channel_id=1, source_target_pairs={{0,8},{8,16},{16,24},{24,32},{32,40},{40,48},{48,56},{56,64},{64,7... | collective-permute-start | bytes 786440 | tf_op jit(solution)/shard_map/ppermute | solution.py:45
  31.8 16.9 %collective-permute-start.61 = (bf16[4,2,128,128]{3,2,1,0:T(8,128)(2,1)S(1)}, bf16[4,2,128,128]{3,2,1,0:T(8,128)(2,1)S(1)}, u32[]{:S(2)}, u32[]{:S(2)}) collective-permute-start(bf16[4,2,128,128]{3,2,1,0:T(8,128)(2,1)S(1)} %collective-permute-done.60), channel_id=1, source_target_pairs={{0,8},{8,16},{16,24},{24,32},{32,40},{40,48},{48,56},{56,64},{64,7... | collective-permute-start | bytes 786440 | tf_op jit(solution)/shard_map/ppermute | solution.py:45
  37.4 16.9 %collective-permute-start.2 = (bf16[4,2,128,128]{3,2,1,0:T(8,128)(2,1)S(1)}, bf16[4,2,128,128]{3,2,1,0:T(8,128)(2,1)S(1)}, u32[]{:S(2)}, u32[]{:S(2)}) collective-permute-start(bf16[4,2,128,128]{3,2,1,0:T(8,128)(2,1)S(1)} %collective-permute-done.1), channel_id=1, source_target_pairs={{0,8},{8,16},{16,24},{24,32},{32,40},{40,48},{48,56},{56,64},{64,7... | collective-permute-start | bytes 786440 | tf_op jit(solution)/shard_map/ppermute | solution.py:45
  43.0 16.9 %collective-permute-start.17 = (bf16[4,2,128,128]{3,2,1,0:T(8,128)(2,1)S(1)}, bf16[4,2,128,128]{3,2,1,0:T(8,128)(2,1)S(1)}, u32[]{:S(2)}, u32[]{:S(2)}) collective-permute-start(bf16[4,2,128,128]{3,2,1,0:T(8,128)(2,1)S(1)} %collective-permute-done.16), channel_id=1, source_target_pairs={{0,8},{8,16},{16,24},{24,32},{32,40},{40,48},{48,56},{56,64},{64,7... | collective-permute-start | bytes 786440 | tf_op jit(solution)/shard_map/ppermute | solution.py:45
  48.6 16.9 %collective-permute-start.62 = (bf16[4,2,128,128]{3,2,1,0:T(8,128)(2,1)S(1)}, bf16[4,2,128,128]{3,2,1,0:T(8,128)(2,1)S(1)}, u32[]{:S(2)}, u32[]{:S(2)}) collective-permute-start(bf16[4,2,128,128]{3,2,1,0:T(8,128)(2,1)S(1)} %collective-permute-done.61), channel_id=1, source_target_pairs={{0,8},{8,16},{16,24},{24,32},{32,40},{40,48},{48,56},{56,64},{64,7... | collective-permute-start | bytes 786440 | tf_op jit(solution)/shard_map/ppermute | solution.py:45
  59.9 16.9 %collective-permute-start.18 = (bf16[4,2,128,128]{3,2,1,0:T(8,128)(2,1)S(1)}, bf16[4,2,128,128]{3,2,1,0:T(8,128)(2,1)S(1)}, u32[]{:S(2)}, u32[]{:S(2)}) collective-permute-start(bf16[4,2,128,128]{3,2,1,0:T(8,128)(2,1)S(1)} %collective-permute-done.17), channel_id=1, source_target_pairs={{0,8},{8,16},{16,24},{24,32},{32,40},{40,48},{48,56},{56,64},{64,7... | collective-permute-start | bytes 786440 | tf_op jit(solution)/shard_map/ppermute | solution.py:45
  65.5 16.9 %collective-permute-start.63 = (bf16[4,2,128,128]{3,2,1,0:T(8,128)(2,1)S(1)}, bf16[4,2,128,128]{3,2,1,0:T(8,128)(2,1)S(1)}, u32[]{:S(2)}, u32[]{:S(2)}) collective-permute-start(bf16[4,2,128,128]{3,2,1,0:T(8,128)(2,1)S(1)} %collective-permute-done.62), channel_id=1, source_target_pairs={{0,8},{8,16},{16,24},{24,32},{32,40},{40,48},{48,56},{56,64},{64,7... | collective-permute-start | bytes 786440 | tf_op jit(solution)/shard_map/ppermute | solution.py:45
  76.7 16.9 %collective-permute-start.19 = (bf16[4,2,128,128]{3,2,1,0:T(8,128)(2,1)S(1)}, bf16[4,2,128,128]{3,2,1,0:T(8,128)(2,1)S(1)}, u32[]{:S(2)}, u32[]{:S(2)}) collective-permute-start(bf16[4,2,128,128]{3,2,1,0:T(8,128)(2,1)S(1)} %collective-permute-done.18), channel_id=1, source_target_pairs={{0,8},{8,16},{16,24},{24,32},{32,40},{40,48},{48,56},{56,64},{64,7... | collective-permute-start | bytes 786440 | tf_op jit(solution)/shard_map/ppermute | solution.py:45
  88.0 16.9 %collective-permute-start.5 = (bf16[4,2,128,128]{3,2,1,0:T(8,128)(2,1)S(1)}, bf16[4,2,128,128]{3,2,1,0:T(8,128)(2,1)S(1)}, u32[]{:S(2)}, u32[]{:S(2)}) collective-permute-start(bf16[4,2,128,128]{3,2,1,0:T(8,128)(2,1)S(1)} %collective-permute-done.4), channel_id=1, source_target_pairs={{0,8},{8,16},{16,24},{24,32},{32,40},{40,48},{48,56},{56,64},{64,7... | collective-permute-start | bytes 786440 | tf_op jit(solution)/shard_map/ppermute | solution.py:45
  93.6 16.9 %collective-permute-start.20 = (bf16[4,2,128,128]{3,2,1,0:T(8,128)(2,1)S(1)}, bf16[4,2,128,128]{3,2,1,0:T(8,128)(2,1)S(1)}, u32[]{:S(2)}, u32[]{:S(2)}) collective-permute-start(bf16[4,2,128,128]{3,2,1,0:T(8,128)(2,1)S(1)} %collective-permute-done.19), channel_id=1, source_target_pairs={{0,8},{8,16},{16,24},{24,32},{32,40},{40,48},{48,56},{56,64},{64,7... | collective-permute-start | bytes 786440 | tf_op jit(solution)/shard_map/ppermute | solution.py:45
  104.8 16.9 %collective-permute-start.6 = (bf16[4,2,128,128]{3,2,1,0:T(8,128)(2,1)S(1)}, bf16[4,2,128,128]{3,2,1,0:T(8,128)(2,1)S(1)}, u32[]{:S(2)}, u32[]{:S(2)}) collective-permute-start(bf16[4,2,128,128]{3,2,1,0:T(8,128)(2,1)S(1)} %collective-permute-done.5), channel_id=1, source_target_pairs={{0,8},{8,16},{16,24},{24,32},{32,40},{40,48},{48,56},{56,64},{64,7... | collective-permute-start | bytes 786440 | tf_op jit(solution)/shard_map/ppermute | solution.py:45
  110.4 16.9 %collective-permute-start.21 = (bf16[4,2,128,128]{3,2,1,0:T(8,128)(2,1)S(1)}, bf16[4,2,128,128]{3,2,1,0:T(8,128)(2,1)S(1)}, u32[]{:S(2)}, u32[]{:S(2)}) collective-permute-start(bf16[4,2,128,128]{3,2,1,0:T(8,128)(2,1)S(1)} %collective-permute-done.20), channel_id=1, source_target_pairs={{0,8},{8,16},{16,24},{24,32},{32,40},{40,48},{48,56},{56,64},{64,7... | collective-permute-start | bytes 786440 | tf_op jit(solution)/shard_map/ppermute | solution.py:45
  166.6 17.0 %collective-permute-start.69 = (bf16[4,2,128,128]{3,2,1,0:T(8,128)(2,1)S(1)}, bf16[4,2,128,128]{3,2,1,0:T(8,128)(2,1)}, u32[]{:S(2)}, u32[]{:S(2)}) collective-permute-start(bf16[4,2,128,128]{3,2,1,0:T(8,128)(2,1)S(1)} %collective-permute-done.68), channel_id=1, source_target_pairs={{0,8},{8,16},{16,24},{24,32},{32,40},{40,48},{48,56},{56,64},{64,7... | collective-permute-start | bytes 786440 | tf_op jit(solution)/shard_map/ppermute | solution.py:45
  172.2 17.0 %collective-permute-start.10 = (bf16[4,2,128,128]{3,2,1,0:T(8,128)(2,1)S(1)}, bf16[4,2,128,128]{3,2,1,0:T(8,128)(2,1)}, u32[]{:S(2)}, u32[]{:S(2)}) collective-permute-start(bf16[4,2,128,128]{3,2,1,0:T(8,128)(2,1)S(1)} %collective-permute-done.9), channel_id=1, source_target_pairs={{0,8},{8,16},{16,24},{24,32},{32,40},{40,48},{48,56},{56,64},{64,7... | collective-permute-start | bytes 786440 | tf_op jit(solution)/shard_map/ppermute | solution.py:45
  177.8 17.0 %collective-permute-start.25 = (bf16[4,2,128,128]{3,2,1,0:T(8,128)(2,1)S(1)}, bf16[4,2,128,128]{3,2,1,0:T(8,128)(2,1)}, u32[]{:S(2)}, u32[]{:S(2)}) collective-permute-start(bf16[4,2,128,128]{3,2,1,0:T(8,128)(2,1)S(1)} %collective-permute-done.24), channel_id=1, source_target_pairs={{0,8},{8,16},{16,24},{24,32},{32,40},{40,48},{48,56},{56,64},{64,7... | collective-permute-start | bytes 786440 | tf_op jit(solution)/shard_map/ppermute | solution.py:45
  194.8 16.9 %collective-permute-start.26 = (bf16[4,2,128,128]{3,2,1,0:T(8,128)(2,1)}, bf16[4,2,128,128]{3,2,1,0:T(8,128)(2,1)}, u32[]{:S(2)}, u32[]{:S(2)}) collective-permute-start(bf16[4,2,128,128]{3,2,1,0:T(8,128)(2,1)} %collective-permute-done.25), channel_id=1, source_target_pairs={{0,8},{8,16},{16,24},{24,32},{32,40},{40,48},{48,56},{56,64},{64,7... | collective-permute-start | bytes 786440 | tf_op jit(solution)/shard_map/ppermute | solution.py:45
  200.4 16.9 %collective-permute-start.71 = (bf16[4,2,128,128]{3,2,1,0:T(8,128)(2,1)}, bf16[4,2,128,128]{3,2,1,0:T(8,128)(2,1)}, u32[]{:S(2)}, u32[]{:S(2)}) collective-permute-start(bf16[4,2,128,128]{3,2,1,0:T(8,128)(2,1)} %collective-permute-done.70), channel_id=1, source_target_pairs={{0,8},{8,16},{16,24},{24,32},{32,40},{40,48},{48,56},{56,64},{64,7... | collective-permute-start | bytes 786440 | tf_op jit(solution)/shard_map/ppermute | solution.py:45
  206.0 16.9 %collective-permute-start.12 = (bf16[4,2,128,128]{3,2,1,0:T(8,128)(2,1)}, bf16[4,2,128,128]{3,2,1,0:T(8,128)(2,1)}, u32[]{:S(2)}, u32[]{:S(2)}) collective-permute-start(bf16[4,2,128,128]{3,2,1,0:T(8,128)(2,1)} %collective-permute-done.11), channel_id=1, source_target_pairs={{0,8},{8,16},{16,24},{24,32},{32,40},{40,48},{48,56},{56,64},{64,7... | collective-permute-start | bytes 786440 | tf_op jit(solution)/shard_map/ppermute | solution.py:45
  211.7 16.9 %collective-permute-start.27 = (bf16[4,2,128,128]{3,2,1,0:T(8,128)(2,1)}, bf16[4,2,128,128]{3,2,1,0:T(8,128)(2,1)}, u32[]{:S(2)}, u32[]{:S(2)}) collective-permute-start(bf16[4,2,128,128]{3,2,1,0:T(8,128)(2,1)} %collective-permute-done.26), channel_id=1, source_target_pairs={{0,8},{8,16},{16,24},{24,32},{32,40},{40,48},{48,56},{56,64},{64,7... | collective-permute-start | bytes 786440 | tf_op jit(solution)/shard_map/ppermute | solution.py:45
  217.3 16.9 %collective-permute-start.72 = (bf16[4,2,128,128]{3,2,1,0:T(8,128)(2,1)}, bf16[4,2,128,128]{3,2,1,0:T(8,128)(2,1)}, u32[]{:S(2)}, u32[]{:S(2)}) collective-permute-start(bf16[4,2,128,128]{3,2,1,0:T(8,128)(2,1)} %collective-permute-done.71), channel_id=1, source_target_pairs={{0,8},{8,16},{16,24},{24,32},{32,40},{40,48},{48,56},{56,64},{64,7... | collective-permute-start | bytes 786440 | tf_op jit(solution)/shard_map/ppermute | solution.py:45
  222.9 16.9 %collective-permute-start.13 = (bf16[4,2,128,128]{3,2,1,0:T(8,128)(2,1)}, bf16[4,2,128,128]{3,2,1,0:T(8,128)(2,1)}, u32[]{:S(2)}, u32[]{:S(2)}) collective-permute-start(bf16[4,2,128,128]{3,2,1,0:T(8,128)(2,1)} %collective-permute-done.12), channel_id=1, source_target_pairs={{0,8},{8,16},{16,24},{24,32},{32,40},{40,48},{48,56},{56,64},{64,7... | collective-permute-start | bytes 786440 | tf_op jit(solution)/shard_map/ppermute | solution.py:45
  228.5 16.9 %collective-permute-start.28 = (bf16[4,2,128,128]{3,2,1,0:T(8,128)(2,1)}, bf16[4,2,128,128]{3,2,1,0:T(8,128)(2,1)}, u32[]{:S(2)}, u32[]{:S(2)}) collective-permute-start(bf16[4,2,128,128]{3,2,1,0:T(8,128)(2,1)} %collective-permute-done.27), channel_id=1, source_target_pairs={{0,8},{8,16},{16,24},{24,32},{32,40},{40,48},{48,56},{56,64},{64,7... | collective-permute-start | bytes 786440 | tf_op jit(solution)/shard_map/ppermute | solution.py:45
  234.1 16.9 %collective-permute-start.73 = (bf16[4,2,128,128]{3,2,1,0:T(8,128)(2,1)}, bf16[4,2,128,128]{3,2,1,0:T(8,128)(2,1)}, u32[]{:S(2)}, u32[]{:S(2)}) collective-permute-start(bf16[4,2,128,128]{3,2,1,0:T(8,128)(2,1)} %collective-permute-done.72), channel_id=1, source_target_pairs={{0,8},{8,16},{16,24},{24,32},{32,40},{40,48},{48,56},{56,64},{64,7... | collective-permute-start | bytes 786440 | tf_op jit(solution)/shard_map/ppermute | solution.py:45
  239.7 16.9 %collective-permute-start.14 = (bf16[4,2,128,128]{3,2,1,0:T(8,128)(2,1)}, bf16[4,2,128,128]{3,2,1,0:T(8,128)(2,1)}, u32[]{:S(2)}, u32[]{:S(2)}) collective-permute-start(bf16[4,2,128,128]{3,2,1,0:T(8,128)(2,1)} %collective-permute-done.13), channel_id=1, source_target_pairs={{0,8},{8,16},{16,24},{24,32},{32,40},{40,48},{48,56},{56,64},{64,7... | collective-permute-start | bytes 786440 | tf_op jit(solution)/shard_map/ppermute | solution.py:45
  245.4 44.3 %collective-permute-start.29 = (bf16[4,2,128,128]{3,2,1,0:T(8,128)(2,1)}, bf16[4,2,128,128]{3,2,1,0:T(8,128)(2,1)}, u32[]{:S(2)}, u32[]{:S(2)}) collective-permute-start(bf16[4,2,128,128]{3,2,1,0:T(8,128)(2,1)} %collective-permute-done.28), channel_id=1, source_target_pairs={{0,8},{8,16},{16,24},{24,32},{32,40},{40,48},{48,56},{56,64},{64,7... | collective-permute-start | bytes 786440 | tf_op jit(solution)/shard_map/ppermute | solution.py:45
  251.0 16.9 %collective-permute-start.74 = (bf16[4,2,128,128]{3,2,1,0:T(8,128)(2,1)}, bf16[4,2,128,128]{3,2,1,0:T(8,128)(2,1)S(1)}, u32[]{:S(2)}, u32[]{:S(2)}) collective-permute-start(bf16[4,2,128,128]{3,2,1,0:T(8,128)(2,1)} %collective-permute-done.73), channel_id=1, source_target_pairs={{0,8},{8,16},{16,24},{24,32},{32,40},{40,48},{48,56},{56,64},{64,7... | collective-permute-start | bytes 786440 | tf_op jit(solution)/shard_map/ppermute | solution.py:45
  339.6 252.9 %reduce-scatter.11.cloned.1.call-start = ((), (), s32[]{:S(2)}) async-start(), calls=%async_computation.7 | async-start | bytes 4718592 | tf_op jit(solution)/shard_map/reduce_scatter | solution.py:50
  542.7 310.2 %reduce-scatter.9.cloned.1.call-start = ((), (), s32[]{:S(2)}) async-start(), calls=%async_computation.6 | async-start | bytes 4718592 | tf_op jit(solution)/shard_map/reduce_scatter | solution.py:50
  605.1 247.7 %reduce-scatter.7.cloned.1.call-start = ((), (), s32[]{:S(2)}) async-start(), calls=%async_computation.5 | async-start | bytes 4718592 | tf_op jit(solution)/shard_map/reduce_scatter | solution.py:50
  (86 other events, 1992.2 us)
Sparse Core Ops, SparseCore 0:
  339.7 34.3 reduce-scatter.4
  542.8 49.6 reduce-scatter.10
  605.3 36.9 reduce-scatter.8
  770.7 50.0 reduce-scatter.6
